TPU v7x, 256 devices: a whole 4x4x8 slice. The times are simulated.
256 devices in a mesh: row: 32 (over y, x, core), col: 8 (over z).
Axes of the slice: x: 4, y: 4, z: 8, core: 2. Of those that a mesh axis runs over, the one named last changes fastest.
Arguments:
- inputs: bfloat16 [768, 12288], P(None, 'col'), may hold values from -6 to 6
- out_grad: bfloat16 [768, 12288], P(None, 'col'), may hold values from -6 to 6
- pre_act: bfloat16 [768, 24576], P('col', 'row'), may hold values from -8 to 8
- w_in: bfloat16 [12288, 24576], P('col', 'row'), may hold values from -0.0546875 to 0.0546875
- w_out: bfloat16 [24576, 12288], P('row', 'col'), may hold values from -0.0390625 to 0.0390625
Outputs:
- grad_inputs: bfloat16 [768, 12288], P('row', 'col')
- grad_w_in: bfloat16 [12288, 24576], P('col', 'row')
- grad_w_out: bfloat16 [24576, 12288], P('row', 'col')
All inputs are finite; a program needn't handle non-finite values.
Results may differ from a plain program's by a relative error of at most 0.0049.
Values may be sent and summed in bfloat16 or wider, within the bound.
A program may use at most 64 MiB of HBM per device.

v0:
```python
import math
import jax
import jax.numpy as jnp
from jax import lax
from jax.sharding import PartitionSpec as P

coef_c = math.sqrt(2.0 / math.pi)


def gelu_parts(pre_values):
    hval = pre_values.astype(jnp.float32)
    tval = jnp.tanh(coef_c * (hval + 0.044715 * hval * hval * hval))
    activ = 0.5 * hval * (1.0 + tval)
    deriv = 0.5 * (1.0 + tval) + 0.5 * hval * (1.0 - tval * tval) * coef_c * (
        1.0 + 3.0 * 0.044715 * hval * hval
    )
    return (activ, deriv)


def per_device(inputs, out_grad, pre_act, w_in, w_out):
    total_tokens = inputs.shape[0]
    scale_value = 1.0 / math.sqrt(total_tokens)
    block = out_grad
    act_share = lax.psum_scatter(
        lax.dot_general(block, w_out, (((1,), (1,)), ((), ())), preferred_element_type=jnp.float32),
        "col",
        scatter_dimension=0,
        tiled=True,
    )
    local_act, local_deriv = gelu_parts(pre_act)
    hid_share = (act_share * local_deriv).astype(jnp.bfloat16)
    activ_all, hid_all = (
        lax.all_gather(local_act.astype(jnp.bfloat16), "col", axis=0, tiled=True),
        lax.all_gather(hid_share, "col", axis=0, tiled=True),
    )
    grad_w_out = lax.dot_general(
        activ_all, out_grad, (((0,), (0,)), ((), ())), preferred_element_type=jnp.float32
    )
    grad_w_out = (grad_w_out * scale_value).astype(jnp.bfloat16)
    grad_w_in = lax.dot_general(
        inputs, hid_all, (((0,), (0,)), ((), ())), preferred_element_type=jnp.float32
    )
    grad_w_in = (grad_w_in * scale_value).astype(jnp.bfloat16)
    block = hid_all
    grad_inputs = lax.psum_scatter(
        lax.dot_general(block, w_in, (((1,), (1,)), ((), ())), preferred_element_type=jnp.float32),
        "row",
        scatter_dimension=0,
        tiled=True,
    )
    return (grad_inputs.astype(jnp.bfloat16), grad_w_in, grad_w_out)


def solution(mesh):
    placed = (P(None, "col"), P(None, "col"), P("col", "row"), P("col", "row"), P("row", "col"))
    return jax.shard_map(
        per_device,
        mesh=mesh,
        in_specs=placed,
        out_specs=(P("row", "col"), P("col", "row"), P("row", "col")),
        check_vma=False,
    )
```

profile of v0, /device:TPU:2, one launch (start us, length us, event | category | flops | bytes accessed | tf_op | source)
XLA Modules:
  0.0 241.4 jit_solution(5547403851123938522)
XLA Ops:
  7.2 0.0 copy-start
  7.2 0.0 reduce-scatter.3.cloned.1.call-start
  7.2 1.6 copy-done
  8.8 5.1 %fusion.12 = f32[768,768]{1,0:T(8,128)} fusion(bf16[768,1536]{1,0:T(8,128)(2,1)S(1)} %copy-done, bf16[768,1536]{1,0:T(8,128)(2,1)} %param.9), kind=kOutput, calls=%fused_computation.21 | convolution fusion | flops 1811939328 | bytes 7077888 | tf_op jit(solution)/shard_map/dot_general | solution.py:25
  13.9 0.0 copy-start.1
  13.9 0.0 reduce-scatter.3.cloned.1.call-update
  13.9 0.0 all-gather.3.cloned.1.call-start
  14.0 46.3 %reduce-scatter.3.cloned.1.call-done = f32[96,768]{1,0:T(8,128)} async-done(((f32[768,768]{1,0:T(8,128)}), f32[96,768]{1,0:T(8,128)}) %reduce-scatter.3.cloned.1.call-update) | async-done | bytes 294928 | tf_op jit(solution)/shard_map/reduce_scatter | solution.py:24
  60.3 0.0 copy-done.1
  60.3 1.9 fusion.8
  62.1 0.0 all-gather.3.cloned.1.call-update
  62.2 0.0 all-gather.5.cloned.1.call-start
  62.2 0.7 all-gather.5.cloned.1.call-update
  62.9 0.0 reduce-scatter.5.cloned.1.call-start
  63.0 37.7 %all-gather.3.cloned.1.call-done = bf16[768,768]{1,0:T(8,128)(2,1)} async-done(((bf16[96,768]{1,0:T(8,128)(2,1)}), bf16[768,768]{1,0:T(8,128)(2,1)}) %all-gather.3.cloned.1.call-update) | async-done | bytes 1179664 | tf_op jit(solution)/shard_map/all_gather | solution.py:34
  100.7 6.2 %fusion.13 = f32[768,1536]{1,0:T(8,128)} fusion(bf16[768,768]{1,0:T(8,128)(2,1)} %all-gather.3.cloned.1.call-done, bf16[1536,768]{1,0:T(8,128)(2,1)} %param.8), kind=kOutput, calls=%fused_computation.22 | convolution fusion | flops 1811939328 | bytes 8257536 | tf_op jit(solution)/shard_map/dot_general | solution.py:46
  106.9 0.0 copy-start.2
  106.9 0.0 reduce-scatter.5.cloned.1.call-update
  106.9 1.2 copy-done.2
  108.1 5.1 %fusion = bf16[1536,768]{0,1:T(8,128)(2,1)} fusion(bf16[768,768]{1,0:T(8,128)(2,1)S(1)} %copy-done.2, bf16[768,1536]{1,0:T(8,128)(2,1)} %param.5), kind=kOutput, calls=%fused_computation.2 | convolution fusion | flops 1814298624 | bytes 5898240 | tf_op jit(solution)/shard_map/dot_general | solution.py:40
  113.2 4.3 %copy.8 = bf16[1536,768]{1,0:T(8,128)(2,1)} copy(bf16[1536,768]{0,1:T(8,128)(2,1)} %fusion) | data formatting | bytes 4718592
  117.5 22.2 %all-gather.5.cloned.1.call-done = bf16[768,768]{1,0:T(8,128)(2,1)} async-done(((bf16[96,768]{1,0:T(8,128)(2,1)}), bf16[768,768]{1,0:T(8,128)(2,1)}) %all-gather.5.cloned.1.call-update) | async-done | bytes 1179664 | tf_op jit(solution)/shard_map/all_gather | solution.py:33
  139.7 4.7 %multiply_convert_fusion = bf16[768,1536]{1,0:T(8,128)(2,1)} fusion(bf16[768,768]{1,0:T(8,128)(2,1)} %all-gather.5.cloned.1.call-done, bf16[768,1536]{1,0:T(8,128)(2,1)S(1)} %copy-done), kind=kOutput, calls=%fused_computation | convolution fusion | flops 1814298624 | bytes 5898240 | tf_op jit(solution)/shard_map/dot_general | solution.py:36
  144.4 88.9 %reduce-scatter.5.cloned.1.call-done = f32[24,1536]{1,0:T(8,128)} async-done(((f32[768,1536]{1,0:T(8,128)}), f32[24,1536]{1,0:T(8,128)}) %reduce-scatter.5.cloned.1.call-update) | async-done | bytes 147472 | tf_op jit(solution)/shard_map/reduce_scatter | solution.py:45
  233.3 1.6 convert_element_type.23
Async XLA Ops:
  7.2 1.7 copy-start
  7.2 53.1 %reduce-scatter.3.cloned.1.call-start = ((), (), s32[]{:S(2)}) async-start(), calls=%async_computation.2 | async-start | bytes 2654208 | tf_op jit(solution)/shard_map/reduce_scatter | solution.py:24
  13.9 46.3 %copy-start.1 = (bf16[96,768]{1,0:T(8,128)(2,1)S(1)}, bf16[96,768]{1,0:T(8,128)(2,1)}, u32[]{:S(2)}) copy-start(bf16[96,768]{1,0:T(8,128)(2,1)} %param.7) | copy-start | bytes 442372
  13.9 86.7 %all-gather.3.cloned.1.call-start = ((), (), s32[]{:S(2)}) async-start(), calls=%async_computation.3 | async-start | bytes 1327104 | tf_op jit(solution)/shard_map/all_gather | solution.py:34
  62.2 77.6 %all-gather.5.cloned.1.call-start = ((), (), s32[]{:S(2)}) async-start(), calls=%async_computation.5 | async-start | bytes 1327104 | tf_op jit(solution)/shard_map/all_gather | solution.py:33
  62.9 170.4 %reduce-scatter.5.cloned.1.call-start = ((), (), s32[]{:S(2)}) async-start(), calls=%async_computation.4 | async-start | bytes 4866048 | tf_op jit(solution)/shard_map/reduce_scatter | solution.py:45
  106.9 1.3 copy-start.2
Sparse Core Ops, SparseCore 0:
  14.1 46.1 reduce-scatter.2
  62.6 37.9 all-gather.2
  102.5 37.2 all-gather.4
  143.6 89.6 reduce-scatter.4
where the time goes:
time: 242 us; the launch traced here: 241 us
  waiting for transfers between devices  196 us (81%)
  matrix products  21.1 us (9%)
  between operations  13.8 us (6%)
  local copies, waits for them, and re-layouts  7.13 us (3%)
  other arithmetic  3.43 us (1%)
    reduce_scatter x1, waiting for transfers between devices, per_device(): lax.psum_scatter(lax.dot_general(block, w_in, (((1,), (1,)), ((), ())), p...  88.9 us
    reduce_scatter x1, waiting for transfers between devices, per_device(): lax.psum_scatter(lax.dot_general(block, w_out, (((1,), (1,)), ((), ())),...  46.3 us
    all_gather x1, waiting for transfers between devices, per_device(): lax.all_gather(hid_share, 'col', axis=0, tiled=True)  37.7 us
    all_gather x1, waiting for transfers between devices, per_device(): lax.all_gather(local_act.astype(jnp.bfloat16), 'col', axis=0, tiled=True)  22.2 us
    unnamed x7, local copies, waits for them, and re-layouts  7.13 us
    dot_general x1, matrix products, per_device(): lax.dot_general(block, w_in, (((1,), (1,)), ((), ())), preferred_element_...  6.2 us
    dot_general x1, matrix products, per_device(): lax.dot_general(inputs, hid_all, (((0,), (0,)), ((), ())), preferred_elem...  5.1 us
    dot_general x1, matrix products, per_device(): lax.dot_general(block, w_out, (((1,), (1,)), ((), ())), preferred_element...  5.09 us
  transfers between devices with their start and end apart: 4, of which 4 were waited for; matrix products, arithmetic and copies ran while one was open for 8% of the time, Pallas kernels for 0%

commit v1 on v0

--- a/solution.py
+++ b/solution.py
@@ -29,9 +29,13 @@
     )
     local_act, local_deriv = gelu_parts(pre_act)
     hid_share = (act_share * local_deriv).astype(jnp.bfloat16)
+    scan_body = lambda block_here: jnp.concatenate(
+        jax.lax.all_to_all(jnp.stack(jax.lax.axis_size("col") * [block_here], axis=0), "col", 0, 0),
+        axis=0,
+    )
     activ_all, hid_all = (
         lax.all_gather(local_act.astype(jnp.bfloat16), "col", axis=0, tiled=True),
-        lax.all_gather(hid_share, "col", axis=0, tiled=True),
+        scan_body(hid_share),
     )
     grad_w_out = lax.dot_general(
         activ_all, out_grad, (((0,), (0,)), ((), ())), preferred_element_type=jnp.float32

time: 242 us -> 216 us (0.89)
  waiting for transfers between devices: 196 us -> 166 us
  starting transfers between devices: 0.16 us -> 5.09 us
    all_gather x1 -> x0, waiting for transfers between devices: 37.7 us -> none  [per_device(): lax.all_gather(hid_share, 'col', axis=0, tiled=True)]
    all_to_all x0 -> x1, waiting for transfers between devices: none -> 30.3 us  [per_device(): jax.lax.all_to_all(jnp.stack(jax.lax.axis_size('col') * [block_here], axi...]
    all_gather x1, waiting for transfers between devices: 22.2 us -> 0.01 us  [per_device(): lax.all_gather(local_act.astype(jnp.bfloat16), 'col', axis=0, tiled=True)]
    all_to_all x0 -> x1, starting transfers between devices: none -> 4.97 us  [per_device(): jax.lax.all_to_all(jnp.stack(jax.lax.axis_size('col') * [block_here], axi...]
    unnamed x7 -> x5, local copies, waits for them, and re-layouts: 7.13 us -> 5.89 us
  transfers between devices with their start and end apart: 4 -> 4, of which waited for: 4 -> 3; matrix products, arithmetic and copies ran while one was open for 8% -> 9% of each run, Pallas kernels for 0% -> 0%
where the time goes in v1:
time: 216 us; the launch traced here: 215 us
  waiting for transfers between devices  166 us (77%)
  matrix products  20.7 us (10%)
  between operations  13.8 us (6%)
  local copies, waits for them, and re-layouts  6.98 us (3%)
  starting transfers between devices  5.09 us (2%)
  other arithmetic  3.39 us (2%)
    reduce_scatter x1, waiting for transfers between devices, per_device(): lax.psum_scatter(lax.dot_general(block, w_in, (((1,), (1,)), ((), ())), p...  88.2 us
    reduce_scatter x1, waiting for transfers between devices, per_device(): lax.psum_scatter(lax.dot_general(block, w_out, (((1,), (1,)), ((), ())),...  46.3 us
    all_to_all x1, waiting for transfers between devices, per_device(): jax.lax.all_to_all(jnp.stack(jax.lax.axis_size('col') * [block_here], axi...  30.3 us
    unnamed x5, local copies, waits for them, and re-layouts  5.89 us
    dot_general x1, matrix products, per_device(): lax.dot_general(block, w_in, (((1,), (1,)), ((), ())), preferred_element_...  5.82 us
    dot_general x1, matrix products, per_device(): lax.dot_general(inputs, hid_all, (((0,), (0,)), ((), ())), preferred_elem...  5.12 us
    dot_general x1, matrix products, per_device(): lax.dot_general(block, w_out, (((1,), (1,)), ((), ())), preferred_element...  5.09 us
    all_to_all x1, starting transfers between devices, per_device(): jax.lax.all_to_all(jnp.stack(jax.lax.axis_size('col') * [block_here], axi...  4.97 us
  transfers between devices with their start and end apart: 4, of which 3 were waited for; matrix products, arithmetic and copies ran while one was open for 9% of the time, Pallas kernels for 0%

profile of v1, /device:TPU:2, one launch (start us, length us, event | category | flops | bytes accessed | tf_op | source)
XLA Modules:
  0.0 215.5 jit_solution(4363516967143983496)
XLA Ops:
  7.2 0.0 copy-start
  7.2 0.0 reduce-scatter.3.cloned.1.call-start
  7.2 1.6 copy-done
  8.8 5.1 %fusion.12 = f32[768,768]{1,0:T(8,128)} fusion(bf16[768,1536]{1,0:T(8,128)(2,1)S(1)} %copy-done, bf16[768,1536]{1,0:T(8,128)(2,1)} %param.9), kind=kOutput, calls=%fused_computation.21 | convolution fusion | flops 1811939328 | bytes 7077888 | tf_op jit(solution)/shard_map/dot_general | solution.py:25
  13.9 0.0 copy-start.1
  13.9 0.0 reduce-scatter.3.cloned.1.call-update
  13.9 46.3 %reduce-scatter.3.cloned.1.call-done = f32[96,768]{1,0:T(8,128)} async-done(((f32[768,768]{1,0:T(8,128)}), f32[96,768]{1,0:T(8,128)}) %reduce-scatter.3.cloned.1.call-update) | async-done | bytes 294928 | tf_op jit(solution)/shard_map/reduce_scatter | solution.py:24
  60.3 0.0 copy-done.1
  60.3 1.8 fusion.8
  62.1 1.1 stack.2
  63.2 5.0 %all-to-all-start = ((bf16[8,96,768]{2,1,0:T(8,128)(2,1)}), bf16[8,96,768]{2,1,0:T(8,128)(2,1)S(1)}, u32[]{:S(2)}, u32[]{:S(2)}) async-start(bf16[8,96,768]{2,1,0:T(8,128)(2,1)} %stack.2), calls=%async_computation.1 | async-start | bytes 2359296 | tf_op jit(solution)/shard_map/all_to_all | solution.py:33
  68.2 0.0 all-gather.2.cloned.1.call-start
  68.2 0.7 all-gather.2.cloned.1.call-update
  68.9 0.0 reduce-scatter.5.cloned.1.call-start
  69.0 30.3 %all-to-all-done = bf16[8,96,768]{2,1,0:T(8,128)(2,1)S(1)} async-done(((bf16[8,96,768]{2,1,0:T(8,128)(2,1)}), bf16[8,96,768]{2,1,0:T(8,128)(2,1)S(1)}, u32[]{:S(2)}, u32[]{:S(2)}) %all-to-all-start) | async-done | bytes 1179680 | tf_op jit(solution)/shard_map/all_to_all | solution.py:33
  99.3 5.8 %fusion.13 = f32[768,1536]{1,0:T(8,128)} fusion(bf16[768,768]{1,0:T(8,128)(2,1)S(1)} %bitcast.11, bf16[1536,768]{1,0:T(8,128)(2,1)} %param.8), kind=kOutput, calls=%fused_computation.22 | convolution fusion | flops 1811939328 | bytes 8257536 | tf_op jit(solution)/shard_map/dot_general | solution.py:50
  105.1 0.0 reduce-scatter.5.cloned.1.call-update
  105.2 5.1 %fusion = bf16[1536,768]{0,1:T(8,128)(2,1)} fusion(bf16[768,768]{1,0:T(8,128)(2,1)S(1)} %bitcast.12, bf16[768,1536]{1,0:T(8,128)(2,1)} %param.5), kind=kOutput, calls=%fused_computation.2 | convolution fusion | flops 1814298624 | bytes 5898240 | tf_op jit(solution)/shard_map/dot_general | solution.py:44
  110.3 4.3 %copy.8 = bf16[1536,768]{1,0:T(8,128)(2,1)} copy(bf16[1536,768]{0,1:T(8,128)(2,1)} %fusion) | data formatting | bytes 4718592
  114.6 0.0 all-gather.2.cloned.1.call-done
  114.6 4.7 %multiply_convert_fusion = bf16[768,1536]{1,0:T(8,128)(2,1)} fusion(bf16[768,768]{1,0:T(8,128)(2,1)} %all-gather.2.cloned.1.call-done, bf16[768,1536]{1,0:T(8,128)(2,1)S(1)} %copy-done), kind=kOutput, calls=%fused_computation | convolution fusion | flops 1814298624 | bytes 5898240 | tf_op jit(solution)/shard_map/dot_general | solution.py:40
  119.3 88.2 %reduce-scatter.5.cloned.1.call-done = f32[24,1536]{1,0:T(8,128)} async-done(((f32[768,1536]{1,0:T(8,128)}), f32[24,1536]{1,0:T(8,128)}) %reduce-scatter.5.cloned.1.call-update) | async-done | bytes 147472 | tf_op jit(solution)/shard_map/reduce_scatter | solution.py:49
  207.4 1.6 convert_element_type.23
Async XLA Ops:
  7.2 1.7 copy-start
  7.2 53.1 %reduce-scatter.3.cloned.1.call-start = ((), (), s32[]{:S(2)}) async-start(), calls=%async_computation.3 | async-start | bytes 2654208 | tf_op jit(solution)/shard_map/reduce_scatter | solution.py:24
  13.9 46.3 %copy-start.1 = (bf16[96,768]{1,0:T(8,128)(2,1)S(1)}, bf16[96,768]{1,0:T(8,128)(2,1)}, u32[]{:S(2)}) copy-start(bf16[96,768]{1,0:T(8,128)(2,1)} %param.7) | copy-start | bytes 442372
  63.2 36.1 %all-to-all-start = ((bf16[8,96,768]{2,1,0:T(8,128)(2,1)}), bf16[8,96,768]{2,1,0:T(8,128)(2,1)S(1)}, u32[]{:S(2)}, u32[]{:S(2)}) async-start(bf16[8,96,768]{2,1,0:T(8,128)(2,1)} %stack.2), calls=%async_computation.1 | async-start | bytes 2359296 | tf_op jit(solution)/shard_map/all_to_all | solution.py:33
  68.2 46.4 %all-gather.2.cloned.1.call-start = ((), (), s32[]{:S(2)}) async-start(), calls=%async_computation.5 | async-start | bytes 1327104 | tf_op jit(solution)/shard_map/all_gather | solution.py:37
  68.9 138.5 %reduce-scatter.5.cloned.1.call-start = ((), (), s32[]{:S(2)}) async-start(), calls=%async_computation.4 | async-start | bytes 4866048 | tf_op jit(solution)/shard_map/reduce_scatter | solution.py:49
Sparse Core Ops, SparseCore 0:
  14.1 46.1 reduce-scatter.2
  70.8 42.5 all-gather.1
  117.4 89.9 reduce-scatter.4
